TPU v7x, 32 devices: a whole 2x2x4 slice. The times are simulated.
32 devices in a mesh: rows: 8 (over z, x), cols: 4 (over y, core).
Axes of the slice: x: 2, y: 2, z: 4, core: 2. Of those that a mesh axis runs over, the one named last changes fastest.
Arguments:
- source_coords: float32 [3, 128, 128], P(None, ('rows', 'cols')), may hold values from -2 to 5
- target_coords: float32 [3, 128, 128], P(None, ('rows', 'cols')), may hold values from -2 to 5
- source_logmass: float32 [128, 128], P(('rows', 'cols')), may hold values from -4 to 134
- target_logmass: float32 [128, 128], P(('rows', 'cols')), may hold values from -4 to 134
- pair_targets: int32 [128, 8], P(('rows', 'cols')), may hold values from 0 to 127, as said below
- pair_counts: int32 [128], P(('rows', 'cols')), may hold values from 1 to 8
Outputs:
- source_potential: float32 [128, 128], P(('rows', 'cols'))
- target_potential: float32 [128, 128], P(('rows', 'cols'))
Inputs may be any that keep to these rules, and one draw needn't show every extreme that they name: `pair_targets`: slot 0 of source cluster s holds s itself. Every other used slot names a target cluster held by a device of the same cols index and another rows index. Over the used slots 1 and later of all source clusters of one device, at most 4 name target clusters of one device, and on every device some device is named exactly 4 times. Unused slots hold cluster numbers that are ignored.
All inputs are finite; a program needn't handle non-finite values.
Results may differ from a plain program's by a relative error of at most 0.0003.
Values sent between devices are 32-bit elements; how exact they have to be, the bound alone decides.
No kernel may reach another device: no remote copies, remote signals or barrier semaphores. Data moves between devices by JAX's collectives and lax.ppermute only.
A program may use at most 64 MiB of HBM per device.

v0:
```python
import math
import jax
import jax.numpy as jnp
from jax import lax
from jax.sharding import PartitionSpec as P

C_ITERS = 4
F_ITERS = 2
NEGATIVE = -1e30
EPS_C = 0.5
EPS_F = 0.1
RHO = 1.0
TAU_C = RHO / (RHO + EPS_C)
TAU_F = RHO / (RHO + EPS_F)


def joined(part, axis, combine):
    gathered = jax.tree.map(lambda a: lax.all_gather(a, axis), part)

    def take(source):
        return jax.tree.map(lambda a: lax.dynamic_index_in_dim(a, source, 0, False), gathered)

    return lax.fori_loop(
        1, lax.axis_size(axis), lambda source, state: combine(state, take(source)), take(0)
    )


def log_total(values, over_axes):
    highest = jnp.max(values, axis=over_axes, keepdims=True)
    summed = jnp.sum(jnp.exp(values - highest), axis=over_axes)
    return jnp.squeeze(highest, over_axes) + jnp.log(summed)


def coarse_cost(cent_self, cent_other):
    distance = (cent_self[0][:, None] - cent_other[0][None, :]) ** 2
    distance = distance + (cent_self[1][:, None] - cent_other[1][None, :]) ** 2
    distance = distance + (cent_self[2][:, None] - cent_other[2][None, :]) ** 2
    return distance


def coarse_update(pot_other, mass_other, cent_self, cent_other):
    scores = mass_other[None, :] + (pot_other[None, :] - coarse_cost(cent_self, cent_other)) / EPS_C
    return -TAU_C * EPS_C * log_total(scores, 1)


def coarse_blocks(pot_other, mass_other, cent_self, cent_other):
    count = cent_self.shape[1]
    width = math.gcd(count, 8)
    portions = cent_self.reshape(3, count // width, width).transpose(1, 0, 2)
    result = lax.map(
        lambda portion: coarse_update(pot_other, mass_other, portion, cent_other), portions
    )
    return result.reshape(count)


def merge_parts(first, second):
    highest = jnp.maximum(first[0], second[0])
    return (
        highest,
        first[1] * jnp.exp(first[0] - highest) + second[1] * jnp.exp(second[0] - highest),
    )


def column_partials(src_mass, src_pot, src_cent, cent_other):
    count = src_cent.shape[1]
    width = math.gcd(count, 8)
    cent_groups = src_cent.reshape(3, count // width, width).transpose(1, 0, 2)
    mass_groups = src_mass.reshape(count // width, width)
    pot_groups = src_pot.reshape(count // width, width)
    columns = cent_other.shape[1]
    start = (jnp.full((columns,), NEGATIVE, jnp.float32), jnp.zeros((columns,), jnp.float32))

    def step(carry, inputs):
        cent_group, mass_group, pot_group = inputs
        scores = (
            mass_group[:, None] + (pot_group[:, None] - coarse_cost(cent_group, cent_other)) / EPS_C
        )
        highest = jnp.max(scores, axis=0)
        summed = jnp.sum(jnp.exp(scores - highest[None, :]), axis=0)
        return (merge_parts(carry, (highest, summed)), None)

    result, unused = lax.scan(step, start, (cent_groups, mass_groups, pot_groups))
    return result


def pair_cost(src_group, tgt_group):
    distance = (src_group[:, 0, None, :, None] - tgt_group[:, 0, :, None, :]) ** 2
    distance = distance + (src_group[:, 1, None, :, None] - tgt_group[:, 1, :, None, :]) ** 2
    distance = distance + (src_group[:, 2, None, :, None] - tgt_group[:, 2, :, None, :]) ** 2
    return distance


def fine_rows(distance, tgt_mass, tgt_pot, usable):
    scores = tgt_mass[:, :, None, :] + (tgt_pot[:, :, None, :] - distance) / EPS_F
    scores = jnp.where(usable[:, :, None, None], scores, NEGATIVE)
    return -TAU_F * EPS_F * log_total(scores, (1, 3))


def fine_parts(distance, src_mass, src_pot, usable):
    scores = src_mass[:, None, :, None] + (src_pot[:, None, :, None] - distance) / EPS_F
    highest = jnp.max(scores, axis=2)
    summed = jnp.sum(jnp.exp(scores - highest[:, :, None, :]), axis=2)
    highest = jnp.where(usable[:, :, None], highest, NEGATIVE)
    summed = jnp.where(usable[:, :, None], summed, 0.0)
    return (highest, summed)


def local(source_coords, target_coords, source_logmass, target_logmass, pair_targets, pair_counts):
    clusters = source_coords.shape[1]
    points = source_coords.shape[2]
    listed_slots = pair_targets.shape[1]
    row_count = lax.axis_size("rows")
    col_count = lax.axis_size("cols")
    own_index = lax.axis_index("rows") * col_count + lax.axis_index("cols")
    src_cent = jnp.mean(source_coords, axis=2)
    tgt_cent = jnp.mean(target_coords, axis=2)
    src_mass = log_total(source_logmass, 1)
    tgt_mass = log_total(target_logmass, 1)
    every_tgt = lax.all_gather(
        jnp.concatenate([tgt_cent, tgt_mass[None, :]], 0), ("rows", "cols"), axis=1, tiled=True
    )
    tgt_all = jnp.zeros((every_tgt.shape[1],), jnp.float32)
    for sweep in range(C_ITERS):
        src_own = coarse_blocks(tgt_all, every_tgt[3], src_cent, every_tgt[:3])
        highest, summed = column_partials(src_mass, src_own, src_cent, every_tgt[:3])
        highest, summed = joined((highest, summed), ("rows", "cols"), merge_parts)
        tgt_all = -TAU_C * EPS_C * (highest + jnp.log(summed))
    tgt_own = lax.dynamic_slice_in_dim(tgt_all, own_index * clusters, clusters)
    remote = listed_slots - 1
    capacity = 2 * -(-(clusters * remote) // (2 * (row_count - 1)))
    slot_total = row_count * capacity
    remote_ids = pair_targets[:, 1:]
    owner_row = remote_ids // clusters // col_count
    local_ids = remote_ids % clusters
    remote_used = jnp.arange(1, listed_slots)[None, :] < pair_counts[:, None]
    flat_rows = owner_row.reshape(-1)
    flat_used = remote_used.reshape(-1)
    onehot = ((flat_rows[:, None] == jnp.arange(row_count)[None, :]) & flat_used[:, None]).astype(
        jnp.int32
    )
    before = jnp.cumsum(onehot, axis=0) - onehot
    rank_of = jnp.sum(before * onehot, axis=1)
    slot_of = jnp.where(flat_used, flat_rows * capacity + rank_of, slot_total)
    requests = (
        jnp.full((slot_total,), -1, jnp.int32).at[slot_of].set(local_ids.reshape(-1), mode="drop")
    )
    asked = lax.all_to_all(
        requests.reshape(row_count, capacity), "rows", split_axis=0, concat_axis=0, tiled=True
    )
    asked_flat = asked.reshape(-1)
    asked_index = jnp.maximum(asked_flat, 0)
    own_table = jnp.concatenate([target_coords, target_logmass[None, :, :]], 0)
    sent_cells = own_table[:, asked_index].reshape(4, row_count, capacity, points)
    got_cells = lax.all_to_all(sent_cells, "rows", split_axis=1, concat_axis=1, tiled=True)
    cell_table = jnp.concatenate([own_table, got_cells.reshape(4, slot_total, points)], 1)
    pair_index = jnp.concatenate(
        [
            jnp.arange(clusters)[:, None],
            jnp.where(remote_used, clusters + slot_of.reshape(clusters, remote), 0),
        ],
        1,
    )
    pair_cells = cell_table[:, pair_index].transpose(1, 0, 2, 3)
    usable = jnp.arange(listed_slots)[None, :] < pair_counts[:, None]
    matches = jnp.arange(clusters)[:, None] == asked_flat[None, :]
    match_table = matches.astype(jnp.float32)
    group_size = math.gcd(clusters, 4)
    group_count = clusters // group_size

    def in_groups(array):
        return array.reshape((group_count, group_size) + array.shape[1:])

    src_sorted = source_coords.transpose(1, 0, 2)
    pair_mass = pair_cells[:, 3]
    fcost = lax.map(
        lambda inputs: pair_cost(inputs[0], inputs[1][:, :3]),
        (in_groups(src_sorted), in_groups(pair_cells)),
    )
    tgt_now = jnp.broadcast_to(tgt_own[:, None], (clusters, points))
    src_now = jnp.zeros((clusters, points), jnp.float32)
    for sweep in range(F_ITERS):
        sent_pot = tgt_now[asked_index].reshape(row_count, capacity, points)
        got_pot = lax.all_to_all(sent_pot, "rows", split_axis=0, concat_axis=0, tiled=True)
        pot_table = jnp.concatenate([tgt_now, got_pot.reshape(slot_total, points)], 0)
        pair_pot = pot_table[pair_index]

        def rows_of(inputs):
            cost_group, mass_group, pot_group, usable_now = inputs
            return fine_rows(cost_group, mass_group, pot_group, usable_now)

        src_now = lax.map(
            rows_of, (fcost, in_groups(pair_mass), in_groups(pair_pot), in_groups(usable))
        ).reshape(clusters, points)

        def parts_of(inputs):
            cost_group, mass_group, pot_group, usable_now = inputs
            return fine_parts(cost_group, mass_group, pot_group, usable_now)

        highs, sums = lax.map(
            parts_of, (fcost, in_groups(source_logmass), in_groups(src_now), in_groups(usable))
        )
        highs = highs.reshape(clusters, listed_slots, points)
        sums = sums.reshape(clusters, listed_slots, points)
        back_high = (
            jnp.full((slot_total, points), NEGATIVE, jnp.float32)
            .at[slot_of]
            .set(highs[:, 1:].reshape(-1, points), mode="drop")
        )
        back_sum = (
            jnp.zeros((slot_total, points), jnp.float32)
            .at[slot_of]
            .set(sums[:, 1:].reshape(-1, points), mode="drop")
        )
        got_high, got_sum = (
            lax.all_to_all(
                back_high.reshape(row_count, capacity, points),
                "rows",
                split_axis=0,
                concat_axis=0,
                tiled=True,
            ),
            lax.all_to_all(
                back_sum.reshape(row_count, capacity, points),
                "rows",
                split_axis=0,
                concat_axis=0,
                tiled=True,
            ),
        )
        got_high = got_high.reshape(slot_total, points)
        got_sum = got_sum.reshape(slot_total, points)
        best = jnp.maximum(
            highs[:, 0],
            jnp.max(jnp.where(matches[:, :, None], got_high[None, :, :], NEGATIVE), axis=1),
        )
        scaled = got_sum * jnp.exp(got_high - best[asked_index])
        combined = sums[:, 0] * jnp.exp(highs[:, 0] - best) + jnp.dot(
            match_table, scaled, precision=lax.Precision.HIGHEST
        )
        tgt_now = -TAU_F * EPS_F * (best + jnp.log(combined))
    return (src_now, tgt_now)


def solution(mesh):
    return jax.shard_map(
        local,
        mesh=mesh,
        in_specs=(
            P(None, ("rows", "cols"), None),
            P(None, ("rows", "cols"), None),
            P(("rows", "cols"), None),
            P(("rows", "cols"), None),
            P(("rows", "cols"), None),
            P(("rows", "cols")),
        ),
        out_specs=(P(("rows", "cols"), None), P(("rows", "cols"), None)),
        check_vma=False,
    )
```

profile of v0, /device:TPU:0, one launch (start us, length us, event | category | flops | bytes accessed | tf_op | source)
XLA Modules:
  0.0 449.3 jit_solution(6709271842191339367)
XLA Ops:
  0.7 0.8 broadcast_compare_fusion.1
  1.6 0.8 add_select_fusion.2
  2.5 0.8 broadcast_multiply_fusion.2
  3.8 0.7 scatter_custom_fusion
  4.4 0.7 all_to_all.27
  5.1 7.3 %all-to-all-start = ((s32[8,1,4]{2,1,0:T(1,128)}), s32[8,1,4]{2,1,0:T(1,128)S(1)}, u32[]{:S(2)}, u32[]{:S(2)}) async-start(s32[8,1,4]{2,1,0:T(1,128)} %bitcast.11), calls=%async_computation | async-start | bytes 8192 | tf_op jit(solution)/shard_map/all_to_all | solution.py:147
  13.5 42.1 %all-gather = f32[32,4,4]{2,1,0:T(4,128)S(1)} all-gather(f32[1,4,4]{2,1,0:T(4,128)S(1)} %bitcast.315), channel_id=1, replica_groups=mesh['rows'=8,'cols'=4] {'rows','cols'}, dimensions={0}, use_global_device_ids=true | all-gather | bytes 2112 | tf_op jit(solution)/shard_map/all_gather | solution.py:119
  56.3 36.7 %all-gather.2 = f32[32,1,128]{2,1,0:T(1,128)S(1)} all-gather(f32[1,1,128]{2,1,0:T(1,128)S(1)} %get-tuple-element.865), channel_id=1, replica_groups=mesh['rows'=8,'cols'=4] {'rows','cols'}, dimensions={0}, use_global_device_ids=true | all-gather | bytes 16896 | tf_op jit(solution)/shard_map/all_gather | solution.py:18
  93.0 38.0 %all-gather.1 = f32[32,1,128]{2,1,0:T(1,128)S(1)} all-gather(f32[1,1,128]{2,1,0:T(1,128)S(1)} %get-tuple-element.866), channel_id=1, replica_groups=mesh['rows'=8,'cols'=4] {'rows','cols'}, dimensions={0}, use_global_device_ids=true | all-gather | bytes 16896 | tf_op jit(solution)/shard_map/all_gather | solution.py:18
  131.0 1.4 while.44
  132.9 36.7 %all-gather.4 = f32[32,1,128]{2,1,0:T(1,128)S(1)} all-gather(f32[1,1,128]{2,1,0:T(1,128)S(1)} %get-tuple-element.863), channel_id=1, replica_groups=mesh['rows'=8,'cols'=4] {'rows','cols'}, dimensions={0}, use_global_device_ids=true | all-gather | bytes 16896 | tf_op jit(solution)/shard_map/all_gather | solution.py:18
  169.6 38.0 %all-gather.3 = f32[32,1,128]{2,1,0:T(1,128)S(1)} all-gather(f32[1,1,128]{2,1,0:T(1,128)S(1)} %get-tuple-element.864), channel_id=1, replica_groups=mesh['rows'=8,'cols'=4] {'rows','cols'}, dimensions={0}, use_global_device_ids=true | all-gather | bytes 16896 | tf_op jit(solution)/shard_map/all_gather | solution.py:18
  207.6 1.4 while.45
  209.5 36.7 %all-gather.6 = f32[32,1,128]{2,1,0:T(1,128)S(1)} all-gather(f32[1,1,128]{2,1,0:T(1,128)S(1)} %get-tuple-element.861), channel_id=1, replica_groups=mesh['rows'=8,'cols'=4] {'rows','cols'}, dimensions={0}, use_global_device_ids=true | all-gather | bytes 16896 | tf_op jit(solution)/shard_map/all_gather | solution.py:18
  246.2 38.0 %all-gather.5 = f32[32,1,128]{2,1,0:T(1,128)S(1)} all-gather(f32[1,1,128]{2,1,0:T(1,128)S(1)} %get-tuple-element.862), channel_id=1, replica_groups=mesh['rows'=8,'cols'=4] {'rows','cols'}, dimensions={0}, use_global_device_ids=true | all-gather | bytes 16896 | tf_op jit(solution)/shard_map/all_gather | solution.py:18
  284.2 1.4 while.46
  286.1 36.7 %all-gather.8 = f32[32,1,128]{2,1,0:T(1,128)S(1)} all-gather(f32[1,1,128]{2,1,0:T(1,128)S(1)} %get-tuple-element.859), channel_id=1, replica_groups=mesh['rows'=8,'cols'=4] {'rows','cols'}, dimensions={0}, use_global_device_ids=true | all-gather | bytes 16896 | tf_op jit(solution)/shard_map/all_gather | solution.py:18
  322.7 38.0 %all-gather.7 = f32[32,1,128]{2,1,0:T(1,128)S(1)} all-gather(f32[1,1,128]{2,1,0:T(1,128)S(1)} %get-tuple-element.860), channel_id=1, replica_groups=mesh['rows'=8,'cols'=4] {'rows','cols'}, dimensions={0}, use_global_device_ids=true | all-gather | bytes 16896 | tf_op jit(solution)/shard_map/all_gather | solution.py:18
  360.7 1.4 while.47
  362.7 0.7 fusion.69
  363.6 1.2 gather_fusion.2
  364.7 3.3 all-to-all-start.2
  368.2 1.2 gather_fusion
  369.4 5.1 %all-to-all-done.2 = f32[8,4,128]{2,1,0:T(4,128)S(1)} async-done(((f32[8,4,128]{2,1,0:T(4,128)}), f32[8,4,128]{2,1,0:T(4,128)S(1)}, u32[]{:S(2)}, u32[]{:S(2)}) %all-to-all-start.2) | async-done | bytes 16416 | tf_op jit(solution)/shard_map/all_to_all | solution.py:183
  374.6 3.3 all-to-all-start.1
  378.7 6.1 %all-to-all-done.1 = f32[4,8,4,128]{3,0,2,1:T(4,128)S(1)} async-done(((f32[4,8,4,128]{3,0,2,1:T(4,128)}), f32[4,8,4,128]{3,0,2,1:T(4,128)S(1)}, u32[]{:S(2)}, u32[]{:S(2)}) %all-to-all-start.1) | async-done | bytes 65568 | tf_op jit(solution)/shard_map/all_to_all | solution.py:154
  385.4 1.3 fusion.10
  386.7 1.6 exponential_reduce_fusion.3
  388.4 1.1 fusion.8
  389.5 1.4 exponential_reduce_fusion.2
  391.0 1.2 scatter_custom_fusion.1
  392.2 3.3 all-to-all-start.3
  395.6 1.2 scatter_custom_fusion.2
  396.8 5.3 %all-to-all-done.3 = f32[8,4,128]{2,1,0:T(4,128)S(1)} async-done(((f32[8,4,128]{2,1,0:T(4,128)}), f32[8,4,128]{2,1,0:T(4,128)S(1)}, u32[]{:S(2)}, u32[]{:S(2)}) %all-to-all-start.3) | async-done | bytes 16416 | tf_op jit(solution)/shard_map/all_to_all | solution.py:215
  402.1 3.3 all-to-all-start.4
  406.1 5.8 %all-to-all-done.4 = f32[8,4,128]{2,1,0:T(4,128)S(1)} async-done(((f32[8,4,128]{2,1,0:T(4,128)}), f32[8,4,128]{2,1,0:T(4,128)S(1)}, u32[]{:S(2)}, u32[]{:S(2)}) %all-to-all-start.4) | async-done | bytes 16416 | tf_op jit(solution)/shard_map/all_to_all | solution.py:222
  412.6 8.9 %all_to_all.44 = f32[8,4,128]{2,1,0:T(4,128)S(1)} all-to-all(f32[8,4,128]{2,1,0:T(4,128)S(1)} %bitcast.297), channel_id=1, replica_groups=mesh['rows'=8,'cols'=4] {'rows'}, dimensions={0} | all-to-all | bytes 32768 | tf_op jit(solution)/shard_map/all_to_all | solution.py:183
  422.1 1.3 fusion.11
  423.4 1.6 exponential_reduce_fusion.1
  425.1 1.1 fusion.9
  426.2 1.4 exponential_reduce_fusion
  427.7 1.2 scatter_custom_fusion.3
  428.9 3.3 all-to-all-start.6
  432.3 1.2 scatter_custom_fusion.4
  433.5 5.3 %all-to-all-done.6 = f32[8,4,128]{2,1,0:T(4,128)S(1)} async-done(((f32[8,4,128]{2,1,0:T(4,128)}), f32[8,4,128]{2,1,0:T(4,128)S(1)}, u32[]{:S(2)}, u32[]{:S(2)}) %all-to-all-start.6) | async-done | bytes 16416 | tf_op jit(solution)/shard_map/all_to_all | solution.py:215
  438.8 3.3 all-to-all-start.7
  442.8 5.8 %all-to-all-done.7 = f32[8,4,128]{2,1,0:T(4,128)S(1)} async-done(((f32[8,4,128]{2,1,0:T(4,128)}), f32[8,4,128]{2,1,0:T(4,128)S(1)}, u32[]{:S(2)}, u32[]{:S(2)}) %all-to-all-start.7) | async-done | bytes 16416 | tf_op jit(solution)/shard_map/all_to_all | solution.py:222
  448.6 0.7 fusion.14
  (246 shorter events, 12.7 us)
Async XLA Ops:
  0.6 11.8 %copy-start.5 = (s32[4]{0:T(128)S(1)}, s32[4]{0:T(128)}, u32[]{:S(2)}) copy-start(s32[4]{0:T(128)} %param.19) | copy-start | bytes 52
  1.5 11.0 %copy-start = (f32[4,128]{1,0:T(4,128)S(1)}, f32[4,128]{1,0:T(4,128)}, u32[]{:S(2)}) copy-start(f32[4,128]{1,0:T(4,128)} %param.17) | copy-start | bytes 6148
  1.6 11.0 %copy-start.1 = (f32[4,128]{1,0:T(4,128)S(1)}, f32[4,128]{1,0:T(4,128)}, u32[]{:S(2)}) copy-start(f32[4,128]{1,0:T(4,128)} %param.16) | copy-start | bytes 6148
  2.5 10.6 %copy-start.2 = (f32[3,4,128]{2,1,0:T(4,128)S(1)}, f32[3,4,128]{2,1,0:T(4,128)}, u32[]{:S(2)}) copy-start(f32[3,4,128]{2,1,0:T(4,128)} %param.15) | copy-start | bytes 18436
  3.5 9.7 %copy-start.3 = (f32[3,4,128]{2,1,0:T(4,128)S(1)}, f32[3,4,128]{2,1,0:T(4,128)}, u32[]{:S(2)}) copy-start(f32[3,4,128]{2,1,0:T(4,128)} %param.14) | copy-start | bytes 18436
  5.1 357.1 %all-to-all-start = ((s32[8,1,4]{2,1,0:T(1,128)}), s32[8,1,4]{2,1,0:T(1,128)S(1)}, u32[]{:S(2)}, u32[]{:S(2)}) async-start(s32[8,1,4]{2,1,0:T(1,128)} %bitcast.11), calls=%async_computation | async-start | bytes 8192 | tf_op jit(solution)/shard_map/all_to_all | solution.py:147
  364.7 9.8 %all-to-all-start.2 = ((f32[8,4,128]{2,1,0:T(4,128)}), f32[8,4,128]{2,1,0:T(4,128)S(1)}, u32[]{:S(2)}, u32[]{:S(2)}) async-start(f32[8,4,128]{2,1,0:T(4,128)} %bitcast.63), calls=%async_computation.2 | async-start | bytes 32768 | tf_op jit(solution)/shard_map/all_to_all | solution.py:183
  374.6 10.2 %all-to-all-start.1 = ((f32[4,8,4,128]{3,0,2,1:T(4,128)}), f32[4,8,4,128]{3,0,2,1:T(4,128)S(1)}, u32[]{:S(2)}, u32[]{:S(2)}) async-start(f32[4,8,4,128]{3,0,2,1:T(4,128)} %bitcast.13), calls=%async_computation.1 | async-start | bytes 131072 | tf_op jit(solution)/shard_map/all_to_all | solution.py:154
  392.2 9.9 %all-to-all-start.3 = ((f32[8,4,128]{2,1,0:T(4,128)}), f32[8,4,128]{2,1,0:T(4,128)S(1)}, u32[]{:S(2)}, u32[]{:S(2)}) async-start(f32[8,4,128]{2,1,0:T(4,128)} %bitcast.75), calls=%async_computation.3 | async-start | bytes 32768 | tf_op jit(solution)/shard_map/all_to_all | solution.py:215
  402.1 9.8 %all-to-all-start.4 = ((f32[8,4,128]{2,1,0:T(4,128)}), f32[8,4,128]{2,1,0:T(4,128)S(1)}, u32[]{:S(2)}, u32[]{:S(2)}) async-start(f32[8,4,128]{2,1,0:T(4,128)} %bitcast.78), calls=%async_computation.4 | async-start | bytes 32768 | tf_op jit(solution)/shard_map/all_to_all | solution.py:222
  425.1 2.5 copy-start.4
  428.9 9.9 %all-to-all-start.6 = ((f32[8,4,128]{2,1,0:T(4,128)}), f32[8,4,128]{2,1,0:T(4,128)S(1)}, u32[]{:S(2)}, u32[]{:S(2)}) async-start(f32[8,4,128]{2,1,0:T(4,128)} %bitcast.84), calls=%async_computation.6 | async-start | bytes 32768 | tf_op jit(solution)/shard_map/all_to_all | solution.py:215
  438.8 9.8 %all-to-all-start.7 = ((f32[8,4,128]{2,1,0:T(4,128)}), f32[8,4,128]{2,1,0:T(4,128)S(1)}, u32[]{:S(2)}, u32[]{:S(2)}) async-start(f32[8,4,128]{2,1,0:T(4,128)} %bitcast.87), calls=%async_computation.7 | async-start | bytes 32768 | tf_op jit(solution)/shard_map/all_to_all | solution.py:222
where the time goes:
time: 450 us; the launch traced here: 449 us
  blocking collectives  350 us (78%)
  waiting for transfers between devices  33.4 us (7%)
  starting transfers between devices  27.3 us (6%)
  other arithmetic  21 us (5%)
  local copies, waits for them, and re-layouts  13.9 us (3%)
    all_gather x8, blocking collectives, joined(): gathered = jax.tree.map(lambda a: lax.all_gather(a, axis), part)  299 us
    all_gather x1, blocking collectives, local(): lax.all_gather(jnp.concatenate([tgt_cent, tgt_mass[None, :]], 0), ('rows'...  42.1 us
    all_to_all x2, waiting for transfers between devices, local(): lax.all_to_all(back_sum.reshape(row_count, capacity, points), 'rows', spl...  11.7 us
    all_to_all x2, waiting for transfers between devices, local(): lax.all_to_all(back_high.reshape(row_count, capacity, points), 'rows', sp...  10.5 us
  transfers between devices with their start and end apart: 7, of which 6 were waited for; matrix products, arithmetic and copies ran while one was open for 3% of the time, Pallas kernels for 0%

commit v1 on v0

--- a/solution.py
+++ b/solution.py
@@ -116,9 +116,23 @@
     tgt_cent = jnp.mean(target_coords, axis=2)
     src_mass = log_total(source_logmass, 1)
     tgt_mass = log_total(target_logmass, 1)
-    every_tgt = lax.all_gather(
-        jnp.concatenate([tgt_cent, tgt_mass[None, :]], 0), ("rows", "cols"), axis=1, tiled=True
-    )
+    value = jnp.concatenate([tgt_cent, tgt_mass[None, :]], 0)
+    ways, here, hop = (
+        lax.axis_size(("rows", "cols")),
+        lax.axis_index(("rows", "cols")),
+        value.shape[1],
+    )
+    line, have = (value, 1)
+    while have < ways:
+        line = jnp.concatenate(
+            [
+                line,
+                lax.ppermute(line, ("rows", "cols"), [(d, (d - have) % ways) for d in range(ways)]),
+            ],
+            axis=1,
+        )
+        have = 2 * have
+    every_tgt = jnp.roll(line, here * hop, axis=1)
     tgt_all = jnp.zeros((every_tgt.shape[1],), jnp.float32)
     for sweep in range(C_ITERS):
         src_own = coarse_blocks(tgt_all, every_tgt[3], src_cent, every_tgt[:3])

time: 450 us -> 435 us (0.967)
  blocking collectives: 350 us -> 315 us
  waiting for transfers between devices: 33.4 us -> 45.7 us
  starting transfers between devices: 27.3 us -> 34.1 us
    all_gather x1 -> x0, blocking collectives: 42.1 us -> none  [local(): lax.all_gather(jnp.concatenate([tgt_cent, tgt_mass[None, :]], 0), ('rows'...]
    ppermute x0 -> x5, waiting for transfers between devices: none -> 12.4 us  [local(): lax.ppermute(line, ('rows', 'cols'), [(d, (d - have) % ways) for d in ran...]
    all_gather x8, blocking collectives: 299 us -> 306 us  [joined(): gathered = jax.tree.map(lambda a: lax.all_gather(a, axis), part)]
    ppermute x0 -> x5, starting transfers between devices: none -> 6.86 us  [local(): lax.ppermute(line, ('rows', 'cols'), [(d, (d - have) % ways) for d in ran...]
  transfers between devices with their start and end apart: 7 -> 12, of which waited for: 6 -> 11; matrix products, arithmetic and copies ran while one was open for 3% -> 2% of each run, Pallas kernels for 0% -> 0%
where the time goes in v1:
time: 435 us; the launch traced here: 434 us
  blocking collectives  315 us (72%)
  waiting for transfers between devices  45.7 us (11%)
  starting transfers between devices  34.1 us (8%)
  other arithmetic  21.2 us (5%)
  local copies, waits for them, and re-layouts  14 us (3%)
    all_gather x8, blocking collectives, joined(): gathered = jax.tree.map(lambda a: lax.all_gather(a, axis), part)  306 us
    ppermute x5, waiting for transfers between devices, local(): lax.ppermute(line, ('rows', 'cols'), [(d, (d - have) % ways) for d in ran...  12.4 us
    all_to_all x2, waiting for transfers between devices, local(): lax.all_to_all(back_sum.reshape(row_count, capacity, points), 'rows', spl...  11.7 us
    all_to_all x2, waiting for transfers between devices, local(): lax.all_to_all(back_high.reshape(row_count, capacity, points), 'rows', sp...  10.5 us
    all_to_all x1, blocking collectives, local(): lax.all_to_all(sent_pot, 'rows', split_axis=0, concat_axis=0, tiled=True)  8.94 us
  transfers between devices with their start and end apart: 12, of which 11 were waited for; matrix products, arithmetic and copies ran while one was open for 2% of the time, Pallas kernels for 0%

profile of v1, /device:TPU:0, one launch (start us, length us, event | category | flops | bytes accessed | tf_op | source)
XLA Modules:
  0.0 434.3 jit_solution(1252190427946943397)
XLA Ops:
  1.6 0.8 add_select_fusion.2
  2.3 0.8 broadcast_multiply_fusion.2
  5.0 7.3 %all-to-all-start = ((s32[8,1,4]{2,1,0:T(1,128)}), s32[8,1,4]{2,1,0:T(1,128)S(1)}, u32[]{:S(2)}, u32[]{:S(2)}) async-start(s32[8,1,4]{2,1,0:T(1,128)} %bitcast.11), calls=%async_computation | async-start | bytes 8192 | tf_op jit(solution)/shard_map/all_to_all | solution.py:161
  12.7 4.6 %collective-permute-start = (f32[4,4]{1,0:T(4,128)S(1)}, f32[4,4]{1,0:T(4,128)S(1)}, u32[]{:S(2)}, u32[]{:S(2)}) collective-permute-start(f32[4,4]{1,0:T(4,128)S(1)} %pad_maximum_fusion.4), channel_id=1, source_target_pairs={{0,31},{1,0},{2,1},{3,2},{4,3},{5,4},{6,5},{7,6},{8,7},{9,8},{10,9... | collective-permute-start | bytes 200 | tf_op jit(solution)/shard_map/ppermute | solution.py:130
  18.7 1.1 collective-permute-start.1
  19.9 2.5 collective-permute-done.1
  23.0 3.0 collective-permute-done.2
  27.9 1.8 collective-permute-done.3
  29.8 4.5 %collective-permute-done.4 = f32[4,64]{1,0:T(4,128)S(1)} collective-permute-done((f32[4,64]{1,0:T(4,128)S(1)}, f32[4,64]{1,0:T(4,128)S(1)}, u32[]{:S(2)}, u32[]{:S(2)}) %collective-permute-start.4) | collective-permute-done | bytes 1056 | tf_op jit(solution)/shard_map/ppermute | solution.py:130
  35.0 45.6 %all-gather = f32[32,1,128]{2,1,0:T(1,128)S(1)} all-gather(f32[1,1,128]{2,1,0:T(1,128)S(1)} %get-tuple-element.866), channel_id=1, replica_groups=mesh['rows'=8,'cols'=4] {'rows','cols'}, dimensions={0}, use_global_device_ids=true | all-gather | bytes 16896 | tf_op jit(solution)/shard_map/all_gather | solution.py:18
  80.6 36.7 %all-gather.1 = f32[32,1,128]{2,1,0:T(1,128)S(1)} all-gather(f32[1,1,128]{2,1,0:T(1,128)S(1)} %get-tuple-element.865), channel_id=1, replica_groups=mesh['rows'=8,'cols'=4] {'rows','cols'}, dimensions={0}, use_global_device_ids=true | all-gather | bytes 16896 | tf_op jit(solution)/shard_map/all_gather | solution.py:18
  117.2 1.4 while.44
  119.1 38.0 %all-gather.2 = f32[32,1,128]{2,1,0:T(1,128)S(1)} all-gather(f32[1,1,128]{2,1,0:T(1,128)S(1)} %get-tuple-element.864), channel_id=1, replica_groups=mesh['rows'=8,'cols'=4] {'rows','cols'}, dimensions={0}, use_global_device_ids=true | all-gather | bytes 16896 | tf_op jit(solution)/shard_map/all_gather | solution.py:18
  157.2 36.7 %all-gather.3 = f32[32,1,128]{2,1,0:T(1,128)S(1)} all-gather(f32[1,1,128]{2,1,0:T(1,128)S(1)} %get-tuple-element.863), channel_id=1, replica_groups=mesh['rows'=8,'cols'=4] {'rows','cols'}, dimensions={0}, use_global_device_ids=true | all-gather | bytes 16896 | tf_op jit(solution)/shard_map/all_gather | solution.py:18
  193.8 1.4 while.45
  195.7 38.0 %all-gather.4 = f32[32,1,128]{2,1,0:T(1,128)S(1)} all-gather(f32[1,1,128]{2,1,0:T(1,128)S(1)} %get-tuple-element.862), channel_id=1, replica_groups=mesh['rows'=8,'cols'=4] {'rows','cols'}, dimensions={0}, use_global_device_ids=true | all-gather | bytes 16896 | tf_op jit(solution)/shard_map/all_gather | solution.py:18
  233.8 36.7 %all-gather.5 = f32[32,1,128]{2,1,0:T(1,128)S(1)} all-gather(f32[1,1,128]{2,1,0:T(1,128)S(1)} %get-tuple-element.861), channel_id=1, replica_groups=mesh['rows'=8,'cols'=4] {'rows','cols'}, dimensions={0}, use_global_device_ids=true | all-gather | bytes 16896 | tf_op jit(solution)/shard_map/all_gather | solution.py:18
  270.4 1.4 while.46
  272.3 38.0 %all-gather.6 = f32[32,1,128]{2,1,0:T(1,128)S(1)} all-gather(f32[1,1,128]{2,1,0:T(1,128)S(1)} %get-tuple-element.860), channel_id=1, replica_groups=mesh['rows'=8,'cols'=4] {'rows','cols'}, dimensions={0}, use_global_device_ids=true | all-gather | bytes 16896 | tf_op jit(solution)/shard_map/all_gather | solution.py:18
  310.4 36.7 %all-gather.7 = f32[32,1,128]{2,1,0:T(1,128)S(1)} all-gather(f32[1,1,128]{2,1,0:T(1,128)S(1)} %get-tuple-element.859), channel_id=1, replica_groups=mesh['rows'=8,'cols'=4] {'rows','cols'}, dimensions={0}, use_global_device_ids=true | all-gather | bytes 16896 | tf_op jit(solution)/shard_map/all_gather | solution.py:18
  347.0 1.4 while.47
  348.6 1.2 gather_fusion.2
  349.7 3.3 all-to-all-start.2
  353.2 1.2 gather_fusion
  354.4 5.1 %all-to-all-done.2 = f32[8,4,128]{2,1,0:T(4,128)S(1)} async-done(((f32[8,4,128]{2,1,0:T(4,128)}), f32[8,4,128]{2,1,0:T(4,128)S(1)}, u32[]{:S(2)}, u32[]{:S(2)}) %all-to-all-start.2) | async-done | bytes 16416 | tf_op jit(solution)/shard_map/all_to_all | solution.py:197
  359.5 3.3 all-to-all-start.1
  363.7 6.1 %all-to-all-done.1 = f32[4,8,4,128]{3,0,2,1:T(4,128)S(1)} async-done(((f32[4,8,4,128]{3,0,2,1:T(4,128)}), f32[4,8,4,128]{3,0,2,1:T(4,128)S(1)}, u32[]{:S(2)}, u32[]{:S(2)}) %all-to-all-start.1) | async-done | bytes 65568 | tf_op jit(solution)/shard_map/all_to_all | solution.py:168
  370.4 1.3 fusion.10
  371.7 1.6 exponential_reduce_fusion.3
  373.4 1.1 fusion.8
  374.5 1.4 exponential_reduce_fusion.2
  376.0 1.2 scatter_custom_fusion.1
  377.2 3.3 all-to-all-start.3
  380.6 1.2 scatter_custom_fusion.2
  381.8 5.3 %all-to-all-done.3 = f32[8,4,128]{2,1,0:T(4,128)S(1)} async-done(((f32[8,4,128]{2,1,0:T(4,128)}), f32[8,4,128]{2,1,0:T(4,128)S(1)}, u32[]{:S(2)}, u32[]{:S(2)}) %all-to-all-start.3) | async-done | bytes 16416 | tf_op jit(solution)/shard_map/all_to_all | solution.py:229
  387.0 3.3 all-to-all-start.4
  391.1 5.8 %all-to-all-done.4 = f32[8,4,128]{2,1,0:T(4,128)S(1)} async-done(((f32[8,4,128]{2,1,0:T(4,128)}), f32[8,4,128]{2,1,0:T(4,128)S(1)}, u32[]{:S(2)}, u32[]{:S(2)}) %all-to-all-start.4) | async-done | bytes 16416 | tf_op jit(solution)/shard_map/all_to_all | solution.py:236
  397.6 8.9 %all_to_all.44 = f32[8,4,128]{2,1,0:T(4,128)S(1)} all-to-all(f32[8,4,128]{2,1,0:T(4,128)S(1)} %bitcast.286), channel_id=1, replica_groups=mesh['rows'=8,'cols'=4] {'rows'}, dimensions={0} | all-to-all | bytes 32768 | tf_op jit(solution)/shard_map/all_to_all | solution.py:197
  407.1 1.3 fusion.11
  408.4 1.6 exponential_reduce_fusion.1
  410.1 1.1 fusion.9
  411.2 1.4 exponential_reduce_fusion
  412.7 1.2 scatter_custom_fusion.3
  413.9 3.3 all-to-all-start.6
  417.3 1.2 scatter_custom_fusion.4
  418.5 5.3 %all-to-all-done.6 = f32[8,4,128]{2,1,0:T(4,128)S(1)} async-done(((f32[8,4,128]{2,1,0:T(4,128)}), f32[8,4,128]{2,1,0:T(4,128)S(1)}, u32[]{:S(2)}, u32[]{:S(2)}) %all-to-all-start.6) | async-done | bytes 16416 | tf_op jit(solution)/shard_map/all_to_all | solution.py:229
  423.8 3.3 all-to-all-start.7
  427.8 5.8 %all-to-all-done.7 = f32[8,4,128]{2,1,0:T(4,128)S(1)} async-done(((f32[8,4,128]{2,1,0:T(4,128)}), f32[8,4,128]{2,1,0:T(4,128)S(1)}, u32[]{:S(2)}, u32[]{:S(2)}) %all-to-all-start.7) | async-done | bytes 16416 | tf_op jit(solution)/shard_map/all_to_all | solution.py:236
  (260 shorter events, 18.3 us)
Async XLA Ops:
  0.6 11.7 %copy-start = (f32[4,128]{1,0:T(4,128)S(1)}, f32[4,128]{1,0:T(4,128)}, u32[]{:S(2)}) copy-start(f32[4,128]{1,0:T(4,128)} %param.17) | copy-start | bytes 6148
  0.6 12.0 %copy-start.2 = (f32[3,4,128]{2,1,0:T(4,128)S(1)}, f32[3,4,128]{2,1,0:T(4,128)}, u32[]{:S(2)}) copy-start(f32[3,4,128]{2,1,0:T(4,128)} %param.15) | copy-start | bytes 18436
  3.3 14.1 %copy-start.5 = (s32[4]{0:T(128)S(1)}, s32[4]{0:T(128)}, u32[]{:S(2)}) copy-start(s32[4]{0:T(128)} %param.19) | copy-start | bytes 52
  3.4 14.1 %copy-start.3 = (f32[3,4,128]{2,1,0:T(4,128)S(1)}, f32[3,4,128]{2,1,0:T(4,128)}, u32[]{:S(2)}) copy-start(f32[3,4,128]{2,1,0:T(4,128)} %param.14) | copy-start | bytes 18436
  3.6 14.0 %copy-start.1 = (f32[4,128]{1,0:T(4,128)S(1)}, f32[4,128]{1,0:T(4,128)}, u32[]{:S(2)}) copy-start(f32[4,128]{1,0:T(4,128)} %param.16) | copy-start | bytes 6148
  5.0 21.6 %all-to-all-start = ((s32[8,1,4]{2,1,0:T(1,128)}), s32[8,1,4]{2,1,0:T(1,128)S(1)}, u32[]{:S(2)}, u32[]{:S(2)}) async-start(s32[8,1,4]{2,1,0:T(1,128)} %bitcast.11), calls=%async_computation | async-start | bytes 8192 | tf_op jit(solution)/shard_map/all_to_all | solution.py:161
  12.7 5.9 %collective-permute-start = (f32[4,4]{1,0:T(4,128)S(1)}, f32[4,4]{1,0:T(4,128)S(1)}, u32[]{:S(2)}, u32[]{:S(2)}) collective-permute-start(f32[4,4]{1,0:T(4,128)S(1)} %pad_maximum_fusion.4), channel_id=1, source_target_pairs={{0,31},{1,0},{2,1},{3,2},{4,3},{5,4},{6,5},{7,6},{8,7},{9,8},{10,9... | collective-permute-start | bytes 200 | tf_op jit(solution)/shard_map/ppermute | solution.py:130
  18.7 3.6 collective-permute-start.1
  22.4 3.6 collective-permute-start.2
  26.1 3.6 collective-permute-start.3
  29.7 4.5 %collective-permute-start.4 = (f32[4,64]{1,0:T(4,128)S(1)}, f32[4,64]{1,0:T(4,128)S(1)}, u32[]{:S(2)}, u32[]{:S(2)}) collective-permute-start(f32[4,64]{1,0:T(4,128)S(1)} %concatenate.69), channel_id=1, source_target_pairs={{0,16},{1,17},{2,18},{3,19},{4,20},{5,21},{6,22},{7,23},{8,24},{9,... | collective-permute-start | bytes 3080 | tf_op jit(solution)/shard_map/ppermute | solution.py:130
  349.7 9.8 %all-to-all-start.2 = ((f32[8,4,128]{2,1,0:T(4,128)}), f32[8,4,128]{2,1,0:T(4,128)S(1)}, u32[]{:S(2)}, u32[]{:S(2)}) async-start(f32[8,4,128]{2,1,0:T(4,128)} %bitcast.59), calls=%async_computation.2 | async-start | bytes 32768 | tf_op jit(solution)/shard_map/all_to_all | solution.py:197
  359.5 10.2 %all-to-all-start.1 = ((f32[4,8,4,128]{3,0,2,1:T(4,128)}), f32[4,8,4,128]{3,0,2,1:T(4,128)S(1)}, u32[]{:S(2)}, u32[]{:S(2)}) async-start(f32[4,8,4,128]{3,0,2,1:T(4,128)} %bitcast.13), calls=%async_computation.1 | async-start | bytes 131072 | tf_op jit(solution)/shard_map/all_to_all | solution.py:168
  377.2 9.9 %all-to-all-start.3 = ((f32[8,4,128]{2,1,0:T(4,128)}), f32[8,4,128]{2,1,0:T(4,128)S(1)}, u32[]{:S(2)}, u32[]{:S(2)}) async-start(f32[8,4,128]{2,1,0:T(4,128)} %bitcast.71), calls=%async_computation.3 | async-start | bytes 32768 | tf_op jit(solution)/shard_map/all_to_all | solution.py:229
  387.0 9.8 %all-to-all-start.4 = ((f32[8,4,128]{2,1,0:T(4,128)}), f32[8,4,128]{2,1,0:T(4,128)S(1)}, u32[]{:S(2)}, u32[]{:S(2)}) async-start(f32[8,4,128]{2,1,0:T(4,128)} %bitcast.74), calls=%async_computation.4 | async-start | bytes 32768 | tf_op jit(solution)/shard_map/all_to_all | solution.py:236
  410.0 2.5 copy-start.4
  413.9 9.9 %all-to-all-start.6 = ((f32[8,4,128]{2,1,0:T(4,128)}), f32[8,4,128]{2,1,0:T(4,128)S(1)}, u32[]{:S(2)}, u32[]{:S(2)}) async-start(f32[8,4,128]{2,1,0:T(4,128)} %bitcast.80), calls=%async_computation.6 | async-start | bytes 32768 | tf_op jit(solution)/shard_map/all_to_all | solution.py:229
  423.8 9.8 %all-to-all-start.7 = ((f32[8,4,128]{2,1,0:T(4,128)}), f32[8,4,128]{2,1,0:T(4,128)S(1)}, u32[]{:S(2)}, u32[]{:S(2)}) async-start(f32[8,4,128]{2,1,0:T(4,128)} %bitcast.83), calls=%async_computation.7 | async-start | bytes 32768 | tf_op jit(solution)/shard_map/all_to_all | solution.py:236
